TPU v7x, 32 devices: a whole 2x2x4 slice. The times are simulated.
32 devices in a mesh: row: 8 (over z, core), col: 4 (over y, x).
Axes of the slice: x: 2, y: 2, z: 4, core: 2. Of those that a mesh axis runs over, the one named last changes fastest.
Arguments:
- pivot_inverse: float32 [1024, 1024], P('row'), may hold values from -1 to 2, as said below
- panel: float32 [16, 1024, 1024], P('row', 'col'), may hold values from -1 to 1
- trailing: float32 [160, 1024, 1024], P('row', None, 'col'), may hold values from -6 to 6
- tile_list: int32 [160, 2], P('row'), may hold values from -1 to 15, as said below
Outputs:
- solved_panel: float32 [16, 1024, 1024], P('row', 'col')
- updated: float32 [160, 1024, 1024], P('row', None, 'col')
Inputs may be any that keep to these rules, and one draw needn't show every extreme that they name: `pivot_inverse`: lower triangular, diagonal between 0.5 and 2. `tile_list`: slots t of group g are g * 20 to g * 20 + 19. Column 0 lies in 0 to 1; column 1 is a panel tile or -1 for an empty slot. The live slots of a group come first and name distinct pairs; each group in the first half of the groups holds exactly 6 live slots, each in the second half exactly 20. Empty slots hold 0 in column 0.
All inputs are finite; a program needn't handle non-finite values.
Results may differ from a plain program's by a relative error of at most 0.00007.
Values sent between devices are 32-bit elements; how exact they have to be, the bound alone decides.
A program may use at most 128 MiB of HBM per device.

v0:
```python
import jax
import jax.numpy as jnp
from jax import lax
from jax.sharding import PartitionSpec as P

highest = lax.Precision.HIGHEST


def slot_term(left_tile, right_rows):
    return jnp.einsum("ak,bk->ab", left_tile, right_rows, precision=highest)


def per_device(pivot_inverse, panel, trailing, tile_list):
    full_pivot = lax.all_gather(pivot_inverse, "row", axis=0, tiled=True)
    slice_rows = panel.shape[1]
    tile_order = panel.shape[2]
    solved = jnp.einsum("pak,jk->paj", panel, full_pivot, precision=highest)
    whole_tiles = lax.all_gather(solved, "col", axis=1, tiled=True)
    slices = lax.all_gather(solved, "row", axis=0, tiled=True)
    empty_term = jnp.zeros((tile_order, slice_rows), jnp.float32)

    def owner_slot(listed):
        return lax.cond(
            listed[1] >= 0,
            lambda: slot_term(whole_tiles[listed[0]], slices[jnp.maximum(listed[1], 0)]),
            lambda: empty_term,
        )

    updates = lax.map(owner_slot, tile_list)
    return (solved, trailing - updates)


def solution(mesh):
    placed = (P("row", None), P("row", "col", None), P("row", None, "col"), P("row", None))
    return jax.shard_map(
        per_device,
        mesh=mesh,
        in_specs=placed,
        out_specs=(P("row", "col", None), P("row", None, "col")),
        check_vma=False,
    )
```

profile of v0, /device:TPU:17, one launch (start us, length us, event | category | flops | bytes accessed | tf_op | source)
XLA Modules:
  0.0 549.2 jit_solution(17229575436404876348)
XLA Ops:
  8.0 48.8 %all-gather.4.cloned.1.call-done = f32[1024,1024]{1,0:T(8,128)} async-done(((f32[128,1024]{1,0:T(8,128)}), f32[1024,1024]{1,0:T(8,128)}) %all-gather.4.cloned.1.call-update) | async-done | bytes 4194320 | tf_op jit(solution)/shard_map/all_gather | solution.py:14
  56.8 9.6 %fusion.9 = f32[2,256,1024]{2,1,0:T(8,128)} fusion(f32[2,256,1024]{2,1,0:T(8,128)S(1)} %copy-done, f32[1024,1024]{1,0:T(8,128)} %all-gather.4.cloned.1.call-done), kind=kOutput, calls=%fused_computation.9 | convolution fusion | flops 6442450944 | bytes 8388608 | tf_op jit(solution)/shard_map/pak,jk->paj/dot_general | solution.py:17
  67.3 86.2 %all-gather.6.cloned.1.call-done = f32[2,1024,1024]{2,1,0:T(8,128)} async-done(((f32[2,256,1024]{2,1,0:T(8,128)}), f32[2,1024,1024]{2,1,0:T(8,128)}) %all-gather.6.cloned.1.call-update) | async-done | bytes 8388624 | tf_op jit(solution)/shard_map/all_gather | solution.py:18
  153.5 152.1 %all-gather.8.cloned.1.call-done = f32[16,256,1024]{2,1,0:T(8,128)} async-done(((f32[2,256,1024]{2,1,0:T(8,128)}), f32[16,256,1024]{2,1,0:T(8,128)}) %all-gather.8.cloned.1.call-update) | async-done | bytes 16777232 | tf_op jit(solution)/shard_map/all_gather | solution.py:19
  305.6 215.2 %while.10 = (s32[]{:T(128)}, f32[20,1024,256]{2,1,0:T(8,128)}, s32[20,2]{1,0:T(8,128)S(1)}, f32[2,1024,1024]{2,1,0:T(8,128)}, f32[16,256,1024]{2,1,0:T(8,128)}, /*index=5*/s32[]{:T(128)}, s32[1,1]{1,0:T(1,128)}) while((s32[]{:T(128)}, f32[20,1024,256]{2,1,0:T(8,128)}, s32[20,2]{1,0:T(8,128)S(1)}, f32[2,1024,1024]{2,1,0:T(8,128)}, ...), condition=%wide.region_3.4_spmd, body=%wide.region_0.3_spmd.sunk | while | flops 3221225472 | bytes 8389849 | solution.py:29
  306.7 8.5 %conditional.2 = (f32[1,1024,256]{2,1,0:T(8,128)S(1)}) conditional(s32[]{:T(128)} %bitcast.18, () %tuple.35, (s32[1,2]{1,0:T(1,128)S(1)}, f32[2,1024,1024]{2,1,0:T(8,128)}, f32[16,256,1024]{2,1,0:T(8,128)}) %tuple.36), branch_computations={%region_1.1_spmd, %region_2.2_spmd} | conditional | flops 3221225472 | bytes 6292042 | solution.py:23
  309.7 5.6 %fusion.3 = f32[1,1024,256]{2,1,0:T(8,128)S(1)} fusion(f32[2,1024,1024]{2,1,0:T(8,128)} %get-tuple-element.31, s32[]{:T(128)S(6)} %select_n.0, f32[16,256,1024]{2,1,0:T(8,128)} %get-tuple-element.33, s32[]{:T(128)} %bitcast.2), kind=kOutput, calls=%fused_computation.3 | convolution fusion | flops 3221225472 | bytes 6291972 | tf_op jit(solution)/shard_map/while/body/eval_jaxpr/cond/branch_1_fun/ak,bk->ab/dot_general | solution.py:10
  315.3 1.0 constant_dynamic-update-slice_fusion.2
  317.5 8.5 %conditional.2 = (f32[1,1024,256]{2,1,0:T(8,128)S(1)}) conditional(s32[]{:T(128)} %bitcast.18, () %tuple.35, (s32[1,2]{1,0:T(1,128)S(1)}, f32[2,1024,1024]{2,1,0:T(8,128)}, f32[16,256,1024]{2,1,0:T(8,128)}) %tuple.36), branch_computations={%region_1.1_spmd, %region_2.2_spmd} | conditional | flops 3221225472 | bytes 6292042 | solution.py:23
  320.5 5.6 %fusion.3 = f32[1,1024,256]{2,1,0:T(8,128)S(1)} fusion(f32[2,1024,1024]{2,1,0:T(8,128)} %get-tuple-element.31, s32[]{:T(128)S(6)} %select_n.0, f32[16,256,1024]{2,1,0:T(8,128)} %get-tuple-element.33, s32[]{:T(128)} %bitcast.2), kind=kOutput, calls=%fused_computation.3 | convolution fusion | flops 3221225472 | bytes 6291972 | tf_op jit(solution)/shard_map/while/body/eval_jaxpr/cond/branch_1_fun/ak,bk->ab/dot_general | solution.py:10
  326.0 1.0 constant_dynamic-update-slice_fusion.2
  328.2 8.6 %conditional.2 = (f32[1,1024,256]{2,1,0:T(8,128)S(1)}) conditional(s32[]{:T(128)} %bitcast.18, () %tuple.35, (s32[1,2]{1,0:T(1,128)S(1)}, f32[2,1024,1024]{2,1,0:T(8,128)}, f32[16,256,1024]{2,1,0:T(8,128)}) %tuple.36), branch_computations={%region_1.1_spmd, %region_2.2_spmd} | conditional | flops 3221225472 | bytes 6292042 | solution.py:23
  331.2 5.6 %fusion.3 = f32[1,1024,256]{2,1,0:T(8,128)S(1)} fusion(f32[2,1024,1024]{2,1,0:T(8,128)} %get-tuple-element.31, s32[]{:T(128)S(6)} %select_n.0, f32[16,256,1024]{2,1,0:T(8,128)} %get-tuple-element.33, s32[]{:T(128)} %bitcast.2), kind=kOutput, calls=%fused_computation.3 | convolution fusion | flops 3221225472 | bytes 6291972 | tf_op jit(solution)/shard_map/while/body/eval_jaxpr/cond/branch_1_fun/ak,bk->ab/dot_general | solution.py:10
  336.8 1.0 constant_dynamic-update-slice_fusion.2
  339.0 8.5 %conditional.2 = (f32[1,1024,256]{2,1,0:T(8,128)S(1)}) conditional(s32[]{:T(128)} %bitcast.18, () %tuple.35, (s32[1,2]{1,0:T(1,128)S(1)}, f32[2,1024,1024]{2,1,0:T(8,128)}, f32[16,256,1024]{2,1,0:T(8,128)}) %tuple.36), branch_computations={%region_1.1_spmd, %region_2.2_spmd} | conditional | flops 3221225472 | bytes 6292042 | solution.py:23
  342.0 5.6 %fusion.3 = f32[1,1024,256]{2,1,0:T(8,128)S(1)} fusion(f32[2,1024,1024]{2,1,0:T(8,128)} %get-tuple-element.31, s32[]{:T(128)S(6)} %select_n.0, f32[16,256,1024]{2,1,0:T(8,128)} %get-tuple-element.33, s32[]{:T(128)} %bitcast.2), kind=kOutput, calls=%fused_computation.3 | convolution fusion | flops 3221225472 | bytes 6291972 | tf_op jit(solution)/shard_map/while/body/eval_jaxpr/cond/branch_1_fun/ak,bk->ab/dot_general | solution.py:10
  347.6 1.0 constant_dynamic-update-slice_fusion.2
  349.8 8.6 %conditional.2 = (f32[1,1024,256]{2,1,0:T(8,128)S(1)}) conditional(s32[]{:T(128)} %bitcast.18, () %tuple.35, (s32[1,2]{1,0:T(1,128)S(1)}, f32[2,1024,1024]{2,1,0:T(8,128)}, f32[16,256,1024]{2,1,0:T(8,128)}) %tuple.36), branch_computations={%region_1.1_spmd, %region_2.2_spmd} | conditional | flops 3221225472 | bytes 6292042 | solution.py:23
  352.7 5.6 %fusion.3 = f32[1,1024,256]{2,1,0:T(8,128)S(1)} fusion(f32[2,1024,1024]{2,1,0:T(8,128)} %get-tuple-element.31, s32[]{:T(128)S(6)} %select_n.0, f32[16,256,1024]{2,1,0:T(8,128)} %get-tuple-element.33, s32[]{:T(128)} %bitcast.2), kind=kOutput, calls=%fused_computation.3 | convolution fusion | flops 3221225472 | bytes 6291972 | tf_op jit(solution)/shard_map/while/body/eval_jaxpr/cond/branch_1_fun/ak,bk->ab/dot_general | solution.py:10
  358.3 1.0 constant_dynamic-update-slice_fusion.2
  360.5 8.5 %conditional.2 = (f32[1,1024,256]{2,1,0:T(8,128)S(1)}) conditional(s32[]{:T(128)} %bitcast.18, () %tuple.35, (s32[1,2]{1,0:T(1,128)S(1)}, f32[2,1024,1024]{2,1,0:T(8,128)}, f32[16,256,1024]{2,1,0:T(8,128)}) %tuple.36), branch_computations={%region_1.1_spmd, %region_2.2_spmd} | conditional | flops 3221225472 | bytes 6292042 | solution.py:23
  363.5 5.6 %fusion.3 = f32[1,1024,256]{2,1,0:T(8,128)S(1)} fusion(f32[2,1024,1024]{2,1,0:T(8,128)} %get-tuple-element.31, s32[]{:T(128)S(6)} %select_n.0, f32[16,256,1024]{2,1,0:T(8,128)} %get-tuple-element.33, s32[]{:T(128)} %bitcast.2), kind=kOutput, calls=%fused_computation.3 | convolution fusion | flops 3221225472 | bytes 6291972 | tf_op jit(solution)/shard_map/while/body/eval_jaxpr/cond/branch_1_fun/ak,bk->ab/dot_general | solution.py:10
  369.1 1.0 constant_dynamic-update-slice_fusion.2
  371.3 8.6 %conditional.2 = (f32[1,1024,256]{2,1,0:T(8,128)S(1)}) conditional(s32[]{:T(128)} %bitcast.18, () %tuple.35, (s32[1,2]{1,0:T(1,128)S(1)}, f32[2,1024,1024]{2,1,0:T(8,128)}, f32[16,256,1024]{2,1,0:T(8,128)}) %tuple.36), branch_computations={%region_1.1_spmd, %region_2.2_spmd} | conditional | flops 3221225472 | bytes 6292042 | solution.py:23
  374.2 5.6 %fusion.3 = f32[1,1024,256]{2,1,0:T(8,128)S(1)} fusion(f32[2,1024,1024]{2,1,0:T(8,128)} %get-tuple-element.31, s32[]{:T(128)S(6)} %select_n.0, f32[16,256,1024]{2,1,0:T(8,128)} %get-tuple-element.33, s32[]{:T(128)} %bitcast.2), kind=kOutput, calls=%fused_computation.3 | convolution fusion | flops 3221225472 | bytes 6291972 | tf_op jit(solution)/shard_map/while/body/eval_jaxpr/cond/branch_1_fun/ak,bk->ab/dot_general | solution.py:10
  379.8 1.0 constant_dynamic-update-slice_fusion.2
  382.0 8.5 %conditional.2 = (f32[1,1024,256]{2,1,0:T(8,128)S(1)}) conditional(s32[]{:T(128)} %bitcast.18, () %tuple.35, (s32[1,2]{1,0:T(1,128)S(1)}, f32[2,1024,1024]{2,1,0:T(8,128)}, f32[16,256,1024]{2,1,0:T(8,128)}) %tuple.36), branch_computations={%region_1.1_spmd, %region_2.2_spmd} | conditional | flops 3221225472 | bytes 6292042 | solution.py:23
  385.0 5.6 %fusion.3 = f32[1,1024,256]{2,1,0:T(8,128)S(1)} fusion(f32[2,1024,1024]{2,1,0:T(8,128)} %get-tuple-element.31, s32[]{:T(128)S(6)} %select_n.0, f32[16,256,1024]{2,1,0:T(8,128)} %get-tuple-element.33, s32[]{:T(128)} %bitcast.2), kind=kOutput, calls=%fused_computation.3 | convolution fusion | flops 3221225472 | bytes 6291972 | tf_op jit(solution)/shard_map/while/body/eval_jaxpr/cond/branch_1_fun/ak,bk->ab/dot_general | solution.py:10
  390.6 1.0 constant_dynamic-update-slice_fusion.2
  392.8 8.6 %conditional.2 = (f32[1,1024,256]{2,1,0:T(8,128)S(1)}) conditional(s32[]{:T(128)} %bitcast.18, () %tuple.35, (s32[1,2]{1,0:T(1,128)S(1)}, f32[2,1024,1024]{2,1,0:T(8,128)}, f32[16,256,1024]{2,1,0:T(8,128)}) %tuple.36), branch_computations={%region_1.1_spmd, %region_2.2_spmd} | conditional | flops 3221225472 | bytes 6292042 | solution.py:23
  395.8 5.6 %fusion.3 = f32[1,1024,256]{2,1,0:T(8,128)S(1)} fusion(f32[2,1024,1024]{2,1,0:T(8,128)} %get-tuple-element.31, s32[]{:T(128)S(6)} %select_n.0, f32[16,256,1024]{2,1,0:T(8,128)} %get-tuple-element.33, s32[]{:T(128)} %bitcast.2), kind=kOutput, calls=%fused_computation.3 | convolution fusion | flops 3221225472 | bytes 6291972 | tf_op jit(solution)/shard_map/while/body/eval_jaxpr/cond/branch_1_fun/ak,bk->ab/dot_general | solution.py:10
  401.4 1.0 constant_dynamic-update-slice_fusion.2
  403.6 8.5 %conditional.2 = (f32[1,1024,256]{2,1,0:T(8,128)S(1)}) conditional(s32[]{:T(128)} %bitcast.18, () %tuple.35, (s32[1,2]{1,0:T(1,128)S(1)}, f32[2,1024,1024]{2,1,0:T(8,128)}, f32[16,256,1024]{2,1,0:T(8,128)}) %tuple.36), branch_computations={%region_1.1_spmd, %region_2.2_spmd} | conditional | flops 3221225472 | bytes 6292042 | solution.py:23
  406.5 5.6 %fusion.3 = f32[1,1024,256]{2,1,0:T(8,128)S(1)} fusion(f32[2,1024,1024]{2,1,0:T(8,128)} %get-tuple-element.31, s32[]{:T(128)S(6)} %select_n.0, f32[16,256,1024]{2,1,0:T(8,128)} %get-tuple-element.33, s32[]{:T(128)} %bitcast.2), kind=kOutput, calls=%fused_computation.3 | convolution fusion | flops 3221225472 | bytes 6291972 | tf_op jit(solution)/shard_map/while/body/eval_jaxpr/cond/branch_1_fun/ak,bk->ab/dot_general | solution.py:10
  412.1 1.0 constant_dynamic-update-slice_fusion.2
  414.3 8.6 %conditional.2 = (f32[1,1024,256]{2,1,0:T(8,128)S(1)}) conditional(s32[]{:T(128)} %bitcast.18, () %tuple.35, (s32[1,2]{1,0:T(1,128)S(1)}, f32[2,1024,1024]{2,1,0:T(8,128)}, f32[16,256,1024]{2,1,0:T(8,128)}) %tuple.36), branch_computations={%region_1.1_spmd, %region_2.2_spmd} | conditional | flops 3221225472 | bytes 6292042 | solution.py:23
  417.3 5.6 %fusion.3 = f32[1,1024,256]{2,1,0:T(8,128)S(1)} fusion(f32[2,1024,1024]{2,1,0:T(8,128)} %get-tuple-element.31, s32[]{:T(128)S(6)} %select_n.0, f32[16,256,1024]{2,1,0:T(8,128)} %get-tuple-element.33, s32[]{:T(128)} %bitcast.2), kind=kOutput, calls=%fused_computation.3 | convolution fusion | flops 3221225472 | bytes 6291972 | tf_op jit(solution)/shard_map/while/body/eval_jaxpr/cond/branch_1_fun/ak,bk->ab/dot_general | solution.py:10
  422.9 1.0 constant_dynamic-update-slice_fusion.2
  425.1 8.5 %conditional.2 = (f32[1,1024,256]{2,1,0:T(8,128)S(1)}) conditional(s32[]{:T(128)} %bitcast.18, () %tuple.35, (s32[1,2]{1,0:T(1,128)S(1)}, f32[2,1024,1024]{2,1,0:T(8,128)}, f32[16,256,1024]{2,1,0:T(8,128)}) %tuple.36), branch_computations={%region_1.1_spmd, %region_2.2_spmd} | conditional | flops 3221225472 | bytes 6292042 | solution.py:23
  428.0 5.6 %fusion.3 = f32[1,1024,256]{2,1,0:T(8,128)S(1)} fusion(f32[2,1024,1024]{2,1,0:T(8,128)} %get-tuple-element.31, s32[]{:T(128)S(6)} %select_n.0, f32[16,256,1024]{2,1,0:T(8,128)} %get-tuple-element.33, s32[]{:T(128)} %bitcast.2), kind=kOutput, calls=%fused_computation.3 | convolution fusion | flops 3221225472 | bytes 6291972 | tf_op jit(solution)/shard_map/while/body/eval_jaxpr/cond/branch_1_fun/ak,bk->ab/dot_general | solution.py:10
  433.6 1.0 constant_dynamic-update-slice_fusion.2
  435.8 8.6 %conditional.2 = (f32[1,1024,256]{2,1,0:T(8,128)S(1)}) conditional(s32[]{:T(128)} %bitcast.18, () %tuple.35, (s32[1,2]{1,0:T(1,128)S(1)}, f32[2,1024,1024]{2,1,0:T(8,128)}, f32[16,256,1024]{2,1,0:T(8,128)}) %tuple.36), branch_computations={%region_1.1_spmd, %region_2.2_spmd} | conditional | flops 3221225472 | bytes 6292042 | solution.py:23
  438.8 5.6 %fusion.3 = f32[1,1024,256]{2,1,0:T(8,128)S(1)} fusion(f32[2,1024,1024]{2,1,0:T(8,128)} %get-tuple-element.31, s32[]{:T(128)S(6)} %select_n.0, f32[16,256,1024]{2,1,0:T(8,128)} %get-tuple-element.33, s32[]{:T(128)} %bitcast.2), kind=kOutput, calls=%fused_computation.3 | convolution fusion | flops 3221225472 | bytes 6291972 | tf_op jit(solution)/shard_map/while/body/eval_jaxpr/cond/branch_1_fun/ak,bk->ab/dot_general | solution.py:10
  444.4 1.0 constant_dynamic-update-slice_fusion.2
  446.6 8.5 %conditional.2 = (f32[1,1024,256]{2,1,0:T(8,128)S(1)}) conditional(s32[]{:T(128)} %bitcast.18, () %tuple.35, (s32[1,2]{1,0:T(1,128)S(1)}, f32[2,1024,1024]{2,1,0:T(8,128)}, f32[16,256,1024]{2,1,0:T(8,128)}) %tuple.36), branch_computations={%region_1.1_spmd, %region_2.2_spmd} | conditional | flops 3221225472 | bytes 6292042 | solution.py:23
  449.6 5.6 %fusion.3 = f32[1,1024,256]{2,1,0:T(8,128)S(1)} fusion(f32[2,1024,1024]{2,1,0:T(8,128)} %get-tuple-element.31, s32[]{:T(128)S(6)} %select_n.0, f32[16,256,1024]{2,1,0:T(8,128)} %get-tuple-element.33, s32[]{:T(128)} %bitcast.2), kind=kOutput, calls=%fused_computation.3 | convolution fusion | flops 3221225472 | bytes 6291972 | tf_op jit(solution)/shard_map/while/body/eval_jaxpr/cond/branch_1_fun/ak,bk->ab/dot_general | solution.py:10
  455.1 1.0 constant_dynamic-update-slice_fusion.2
  457.3 8.6 %conditional.2 = (f32[1,1024,256]{2,1,0:T(8,128)S(1)}) conditional(s32[]{:T(128)} %bitcast.18, () %tuple.35, (s32[1,2]{1,0:T(1,128)S(1)}, f32[2,1024,1024]{2,1,0:T(8,128)}, f32[16,256,1024]{2,1,0:T(8,128)}) %tuple.36), branch_computations={%region_1.1_spmd, %region_2.2_spmd} | conditional | flops 3221225472 | bytes 6292042 | solution.py:23
  460.3 5.6 %fusion.3 = f32[1,1024,256]{2,1,0:T(8,128)S(1)} fusion(f32[2,1024,1024]{2,1,0:T(8,128)} %get-tuple-element.31, s32[]{:T(128)S(6)} %select_n.0, f32[16,256,1024]{2,1,0:T(8,128)} %get-tuple-element.33, s32[]{:T(128)} %bitcast.2), kind=kOutput, calls=%fused_computation.3 | convolution fusion | flops 3221225472 | bytes 6291972 | tf_op jit(solution)/shard_map/while/body/eval_jaxpr/cond/branch_1_fun/ak,bk->ab/dot_general | solution.py:10
  465.9 1.0 constant_dynamic-update-slice_fusion.2
  468.1 8.5 %conditional.2 = (f32[1,1024,256]{2,1,0:T(8,128)S(1)}) conditional(s32[]{:T(128)} %bitcast.18, () %tuple.35, (s32[1,2]{1,0:T(1,128)S(1)}, f32[2,1024,1024]{2,1,0:T(8,128)}, f32[16,256,1024]{2,1,0:T(8,128)}) %tuple.36), branch_computations={%region_1.1_spmd, %region_2.2_spmd} | conditional | flops 3221225472 | bytes 6292042 | solution.py:23
  471.1 5.6 %fusion.3 = f32[1,1024,256]{2,1,0:T(8,128)S(1)} fusion(f32[2,1024,1024]{2,1,0:T(8,128)} %get-tuple-element.31, s32[]{:T(128)S(6)} %select_n.0, f32[16,256,1024]{2,1,0:T(8,128)} %get-tuple-element.33, s32[]{:T(128)} %bitcast.2), kind=kOutput, calls=%fused_computation.3 | convolution fusion | flops 3221225472 | bytes 6291972 | tf_op jit(solution)/shard_map/while/body/eval_jaxpr/cond/branch_1_fun/ak,bk->ab/dot_general | solution.py:10
  476.7 1.0 constant_dynamic-update-slice_fusion.2
  478.9 8.6 %conditional.2 = (f32[1,1024,256]{2,1,0:T(8,128)S(1)}) conditional(s32[]{:T(128)} %bitcast.18, () %tuple.35, (s32[1,2]{1,0:T(1,128)S(1)}, f32[2,1024,1024]{2,1,0:T(8,128)}, f32[16,256,1024]{2,1,0:T(8,128)}) %tuple.36), branch_computations={%region_1.1_spmd, %region_2.2_spmd} | conditional | flops 3221225472 | bytes 6292042 | solution.py:23
  481.8 5.6 %fusion.3 = f32[1,1024,256]{2,1,0:T(8,128)S(1)} fusion(f32[2,1024,1024]{2,1,0:T(8,128)} %get-tuple-element.31, s32[]{:T(128)S(6)} %select_n.0, f32[16,256,1024]{2,1,0:T(8,128)} %get-tuple-element.33, s32[]{:T(128)} %bitcast.2), kind=kOutput, calls=%fused_computation.3 | convolution fusion | flops 3221225472 | bytes 6291972 | tf_op jit(solution)/shard_map/while/body/eval_jaxpr/cond/branch_1_fun/ak,bk->ab/dot_general | solution.py:10
  487.4 1.0 constant_dynamic-update-slice_fusion.2
  489.6 8.5 %conditional.2 = (f32[1,1024,256]{2,1,0:T(8,128)S(1)}) conditional(s32[]{:T(128)} %bitcast.18, () %tuple.35, (s32[1,2]{1,0:T(1,128)S(1)}, f32[2,1024,1024]{2,1,0:T(8,128)}, f32[16,256,1024]{2,1,0:T(8,128)}) %tuple.36), branch_computations={%region_1.1_spmd, %region_2.2_spmd} | conditional | flops 3221225472 | bytes 6292042 | solution.py:23
  492.6 5.6 %fusion.3 = f32[1,1024,256]{2,1,0:T(8,128)S(1)} fusion(f32[2,1024,1024]{2,1,0:T(8,128)} %get-tuple-element.31, s32[]{:T(128)S(6)} %select_n.0, f32[16,256,1024]{2,1,0:T(8,128)} %get-tuple-element.33, s32[]{:T(128)} %bitcast.2), kind=kOutput, calls=%fused_computation.3 | convolution fusion | flops 3221225472 | bytes 6291972 | tf_op jit(solution)/shard_map/while/body/eval_jaxpr/cond/branch_1_fun/ak,bk->ab/dot_general | solution.py:10
  498.2 1.0 constant_dynamic-update-slice_fusion.2
  500.4 8.6 %conditional.2 = (f32[1,1024,256]{2,1,0:T(8,128)S(1)}) conditional(s32[]{:T(128)} %bitcast.18, () %tuple.35, (s32[1,2]{1,0:T(1,128)S(1)}, f32[2,1024,1024]{2,1,0:T(8,128)}, f32[16,256,1024]{2,1,0:T(8,128)}) %tuple.36), branch_computations={%region_1.1_spmd, %region_2.2_spmd} | conditional | flops 3221225472 | bytes 6292042 | solution.py:23
  503.3 5.6 %fusion.3 = f32[1,1024,256]{2,1,0:T(8,128)S(1)} fusion(f32[2,1024,1024]{2,1,0:T(8,128)} %get-tuple-element.31, s32[]{:T(128)S(6)} %select_n.0, f32[16,256,1024]{2,1,0:T(8,128)} %get-tuple-element.33, s32[]{:T(128)} %bitcast.2), kind=kOutput, calls=%fused_computation.3 | convolution fusion | flops 3221225472 | bytes 6291972 | tf_op jit(solution)/shard_map/while/body/eval_jaxpr/cond/branch_1_fun/ak,bk->ab/dot_general | solution.py:10
  511.1 8.5 %conditional.2 = (f32[1,1024,256]{2,1,0:T(8,128)S(1)}) conditional(s32[]{:T(128)} %bitcast.18, () %tuple.35, (s32[1,2]{1,0:T(1,128)S(1)}, f32[2,1024,1024]{2,1,0:T(8,128)}, f32[16,256,1024]{2,1,0:T(8,128)}) %tuple.36), branch_computations={%region_1.1_spmd, %region_2.2_spmd} | conditional | flops 3221225472 | bytes 6292042 | solution.py:23
  514.1 5.6 %fusion.3 = f32[1,1024,256]{2,1,0:T(8,128)S(1)} fusion(f32[2,1024,1024]{2,1,0:T(8,128)} %get-tuple-element.31, s32[]{:T(128)S(6)} %select_n.0, f32[16,256,1024]{2,1,0:T(8,128)} %get-tuple-element.33, s32[]{:T(128)} %bitcast.2), kind=kOutput, calls=%fused_computation.3 | convolution fusion | flops 3221225472 | bytes 6291972 | tf_op jit(solution)/shard_map/while/body/eval_jaxpr/cond/branch_1_fun/ak,bk->ab/dot_general | solution.py:10
  520.7 21.9 %sub.3 = f32[20,1024,256]{2,1,0:T(8,128)} subtract(f32[20,1024,256]{2,1,0:T(8,128)} %param.10, f32[20,1024,256]{2,1,0:T(8,128)} %get-tuple-element.43) | non-fusion elementwise | flops 5242880 | bytes 62914560 | tf_op jit(solution)/shard_map/sub | solution.py:30
  (76 shorter events, 27.5 us)
Async XLA Ops:
  7.2 49.6 %copy-start = (f32[2,256,1024]{2,1,0:T(8,128)S(1)}, f32[2,256,1024]{2,1,0:T(8,128)}, u32[]{:S(2)}) copy-start(f32[2,256,1024]{2,1,0:T(8,128)} %param.9) | copy-start | bytes 6291460
  7.2 60.0 %copy-start.2 = (s32[20,2]{0,1:T(2,128)S(1)}, s32[20,2]{0,1:T(2,128)}, u32[]{:S(2)}) copy-start(s32[20,2]{0,1:T(2,128)} %param.11) | copy-start | bytes 484
  7.2 49.6 %all-gather.4.cloned.1.call-start = ((), (), s32[]{:S(2)}) async-start(), calls=%async_computation | async-start | bytes 4718592 | tf_op jit(solution)/shard_map/all_gather | solution.py:14
  7.9 145.6 %all-gather.6.cloned.1.call-start = ((), (), s32[]{:S(2)}) async-start(), calls=%async_computation.1 | async-start | bytes 10485760 | tf_op jit(solution)/shard_map/all_gather | solution.py:18
  66.4 239.1 %all-gather.8.cloned.1.call-start = ((), (), s32[]{:S(2)}) async-start(), calls=%async_computation.2 | async-start | bytes 18874368 | tf_op jit(solution)/shard_map/all_gather | solution.py:19
  520.7 21.9 %copy-start.1 = (f32[2,256,1024]{2,1,0:T(8,128)S(1)}, f32[2,256,1024]{2,1,0:T(8,128)}, u32[]{:S(2)}) copy-start(f32[2,256,1024]{2,1,0:T(8,128)} %param.9) | copy-start | bytes 6291460
Sparse Core Ops, SparseCore 0:
  9.6 47.1 all-gather.3
  66.6 86.8 all-gather.5
  155.7 149.8 all-gather.7
where the time goes:
time: 550 us; the launch traced here: 549 us
  waiting for transfers between devices  288 us (52%)
  matrix products  121 us (22%)
  loops' own time  59 us (11%)
  local copies, waits for them, and re-layouts  44.7 us (8%)
  other arithmetic  21.9 us (4%)
  between operations  13.8 us (3%)
    all_gather x1, waiting for transfers between devices, per_device(): slices = lax.all_gather(solved, 'row', axis=0, tiled=True)  152 us
    dot_general x20, matrix products, slot_term(): return jnp.einsum('ak,bk->ab', left_tile, right_rows, precision=highest)  112 us
    all_gather x1, waiting for transfers between devices, per_device(): whole_tiles = lax.all_gather(solved, 'col', axis=1, tiled=True)  86.2 us
    all_gather x1, waiting for transfers between devices, per_device(): full_pivot = lax.all_gather(pivot_inverse, 'row', axis=0, tiled=True)  48.8 us
    another operation x20, loops' own time, owner_slot(): lax.cond(listed[1] >= 0, lambda: slot_term(whole_tiles[listed[0]], slices...  47.3 us
    sub x1, other arithmetic, per_device(): return (solved, trailing - updates)  21.9 us
    dynamic_update_slice x20, local copies, waits for them, and re-layouts, per_device(): updates = lax.map(owner_slot, tile_list)  20.9 us
    slice x20, local copies, waits for them, and re-layouts, owner_slot(): listed[1]  12.1 us
  transfers between devices with their start and end apart: 3, of which 3 were waited for; matrix products, arithmetic and copies ran while one was open for 0% of the time, Pallas kernels for 0%

commit v1 on v0

--- a/solution.py
+++ b/solution.py
@@ -4,6 +4,27 @@
 from jax.sharding import PartitionSpec as P
 
 highest = lax.Precision.HIGHEST
+
+
+def laid_out(blocks, dim):
+    shape = list(blocks.shape[1:])
+    shape[dim] *= blocks.shape[0]
+    return jnp.moveaxis(blocks, 0, dim).reshape(shape)
+
+
+def doubled(shard, axis):
+    size, index = (lax.axis_size(axis), lax.axis_index(axis))
+    blocks, bit = (shard[None], 1)
+    while bit < size:
+        other = lax.ppermute(blocks, axis, [(i, i ^ bit) for i in range(size)])
+        low = index & bit == 0
+        blocks = jnp.concatenate([jnp.where(low, blocks, other), jnp.where(low, other, blocks)])
+        bit *= 2
+    return blocks
+
+
+def doubled_up(x, axis, dim):
+    return laid_out(doubled(x, axis), dim)
 
 
 def slot_term(left_tile, right_rows):
@@ -15,7 +36,7 @@
     slice_rows = panel.shape[1]
     tile_order = panel.shape[2]
     solved = jnp.einsum("pak,jk->paj", panel, full_pivot, precision=highest)
-    whole_tiles = lax.all_gather(solved, "col", axis=1, tiled=True)
+    whole_tiles = doubled_up(solved, "col", 1)
     slices = lax.all_gather(solved, "row", axis=0, tiled=True)
     empty_term = jnp.zeros((tile_order, slice_rows), jnp.float32)
 

time: 550 us -> 475 us (0.86)
  waiting for transfers between devices: 288 us -> 186 us
  other arithmetic: 21.9 us -> 39.8 us
    all_gather x1, waiting for transfers between devices: 152 us -> 0.01 us  [per_device(): slices = lax.all_gather(solved, 'row', axis=0, tiled=True)]
    ppermute x0 -> x2, waiting for transfers between devices: none -> 136 us  [doubled(): other = lax.ppermute(blocks, axis, [(i, i ^ bit) for i in range(size)])]
    all_gather x1 -> x0, waiting for transfers between devices: 86.2 us -> none  [per_device(): whole_tiles = lax.all_gather(solved, 'col', axis=1, tiled=True)]
    select_n x0 -> x2, other arithmetic: none -> 11 us  [doubled(): jnp.where(low, blocks, other)]
  transfers between devices with their start and end apart: 3 -> 4, of which waited for: 3 -> 3; matrix products, arithmetic and copies ran while one was open for 0% -> 5% of each run, Pallas kernels for 0% -> 0%
where the time goes in v1:
time: 475 us; the launch traced here: 473 us
  waiting for transfers between devices  186 us (39%)
  matrix products  121 us (25%)
  loops' own time  61.7 us (13%)
  local copies, waits for them, and re-layouts  48.1 us (10%)
  other arithmetic  39.8 us (8%)
  between operations  14.1 us (3%)
    ppermute x2, waiting for transfers between devices, doubled(): other = lax.ppermute(blocks, axis, [(i, i ^ bit) for i in range(size)])  136 us
    dot_general x20, matrix products, slot_term(): return jnp.einsum('ak,bk->ab', left_tile, right_rows, precision=highest)  112 us
    another operation x20, loops' own time, owner_slot(): lax.cond(listed[1] >= 0, lambda: slot_term(whole_tiles[listed[0]], slices...  50.1 us
    all_gather x1, waiting for transfers between devices, per_device(): full_pivot = lax.all_gather(pivot_inverse, 'row', axis=0, tiled=True)  48.8 us
    sub x1, other arithmetic, per_device(): return (solved, trailing - updates)  21.9 us
    dynamic_update_slice x20, local copies, waits for them, and re-layouts, per_device(): updates = lax.map(owner_slot, tile_list)  20.9 us
    slice x20, local copies, waits for them, and re-layouts, owner_slot(): listed[1]  11.8 us
    another operation x1, loops' own time, per_device(): updates = lax.map(owner_slot, tile_list)  11.7 us
  transfers between devices with their start and end apart: 4, of which 3 were waited for; matrix products, arithmetic and copies ran while one was open for 5% of the time, Pallas kernels for 0%

profile of v1, /device:TPU:17, one launch (start us, length us, event | category | flops | bytes accessed | tf_op | source)
XLA Modules:
  0.0 473.1 jit_solution(14836523222175139621)
XLA Ops:
  8.0 48.8 %all-gather.3.cloned.1.call-done = f32[1024,1024]{1,0:T(8,128)} async-done(((f32[128,1024]{1,0:T(8,128)}), f32[1024,1024]{1,0:T(8,128)}) %all-gather.3.cloned.1.call-update) | async-done | bytes 4194320 | tf_op jit(solution)/shard_map/all_gather | solution.py:35
  56.8 9.6 %fusion.9 = f32[2,256,1024]{2,1,0:T(8,128)} fusion(f32[2,256,1024]{2,1,0:T(8,128)S(1)} %copy-done, f32[1024,1024]{1,0:T(8,128)} %all-gather.3.cloned.1.call-done), kind=kOutput, calls=%fused_computation.11 | convolution fusion | flops 6442450944 | bytes 8388608 | tf_op jit(solution)/shard_map/pak,jk->paj/dot_general | solution.py:38
  66.4 1.3 collective-permute-start
  67.7 46.0 %collective-permute-done = f32[1,2,256,1024]{3,2,1,0:T(8,128)} collective-permute-done((f32[1,2,256,1024]{3,2,1,0:T(8,128)}, f32[1,2,256,1024]{3,2,1,0:T(8,128)}, u32[]{:S(2)}, u32[]{:S(2)}) %collective-permute-start) | collective-permute-done | bytes 2097184 | tf_op jit(solution)/shard_map/ppermute | solution.py:19
  113.7 2.9 broadcast_select_fusion.3
  116.6 2.6 pad_maximum_fusion
  119.3 1.2 collective-permute-start.1
  120.6 90.0 %collective-permute-done.1 = f32[2,2,256,1024]{3,2,1,0:T(8,128)} collective-permute-done((f32[2,2,256,1024]{3,2,1,0:T(8,128)}, f32[2,2,256,1024]{3,2,1,0:T(8,128)}, u32[]{:S(2)}, u32[]{:S(2)}) %collective-permute-start.1) | collective-permute-done | bytes 4194336 | tf_op jit(solution)/shard_map/ppermute | solution.py:19
  210.6 8.1 %broadcast_select_fusion.1 = (f32[2,2,256,1024]{3,2,1,0:T(8,128)}, f32[2,2,256,1024]{3,2,1,0:T(8,128)}) fusion(f32[2,2,256,1024]{3,2,1,0:T(8,128)} %collective-permute-done.1, pred[]{:T(512)S(6)} %eq.6, f32[1,2,256,1024]{3,2,1,0:T(8,128)} %copy-done.2, f32[1,2,256,1024]{3,2,1,0:T(8,128)S(1)} %get-tuple-element.73), kind=kLoop, calls=%fused_computation.14 | loop fusion | flops 3145728 | bytes 16777216 | tf_op jit(solution)/shard_map/jit(_where)/select_n | solution.py:21
  218.7 4.3 maximum_bitcast_fusion
  223.0 4.1 copy.9
  227.1 217.2 %while.10 = (s32[]{:T(128)}, f32[20,1024,256]{2,1,0:T(8,128)}, s32[20,2]{1,0:T(8,128)S(1)}, f32[2,1024,1024]{2,1,0:T(8,128)}, f32[16,256,1024]{2,1,0:T(8,128)}, /*index=5*/s32[]{:T(128)}, s32[1,1]{1,0:T(1,128)}) while((s32[]{:T(128)}, f32[20,1024,256]{2,1,0:T(8,128)}, s32[20,2]{1,0:T(8,128)S(1)}, f32[2,1024,1024]{2,1,0:T(8,128)}, ...), condition=%wide.region_3.4_spmd, body=%wide.region_0.3_spmd.sunk | while | flops 3221225472 | bytes 8389849 | solution.py:50
  228.2 8.7 %conditional.2 = (f32[1,1024,256]{2,1,0:T(8,128)S(1)}) conditional(s32[]{:T(128)} %bitcast.24, () %tuple.38, (s32[1,2]{1,0:T(1,128)S(1)}, f32[2,1024,1024]{2,1,0:T(8,128)}, f32[16,256,1024]{2,1,0:T(8,128)}) %tuple.39), branch_computations={%region_1.1_spmd, %region_2.2_spmd} | conditional | flops 3221225472 | bytes 6292042 | solution.py:44
  231.3 5.6 %fusion.3 = f32[1,1024,256]{2,1,0:T(8,128)S(1)} fusion(f32[2,1024,1024]{2,1,0:T(8,128)} %get-tuple-element.31, s32[]{:T(128)S(6)} %select_n.21, f32[16,256,1024]{2,1,0:T(8,128)} %get-tuple-element.33, s32[]{:T(128)} %bitcast.2), kind=kOutput, calls=%fused_computation.3 | convolution fusion | flops 3221225472 | bytes 6291972 | tf_op jit(solution)/shard_map/while/body/eval_jaxpr/cond/branch_1_fun/ak,bk->ab/dot_general | solution.py:31
  236.9 1.0 constant_dynamic-update-slice_fusion.2
  239.1 8.7 %conditional.2 = (f32[1,1024,256]{2,1,0:T(8,128)S(1)}) conditional(s32[]{:T(128)} %bitcast.24, () %tuple.38, (s32[1,2]{1,0:T(1,128)S(1)}, f32[2,1024,1024]{2,1,0:T(8,128)}, f32[16,256,1024]{2,1,0:T(8,128)}) %tuple.39), branch_computations={%region_1.1_spmd, %region_2.2_spmd} | conditional | flops 3221225472 | bytes 6292042 | solution.py:44
  242.2 5.6 %fusion.3 = f32[1,1024,256]{2,1,0:T(8,128)S(1)} fusion(f32[2,1024,1024]{2,1,0:T(8,128)} %get-tuple-element.31, s32[]{:T(128)S(6)} %select_n.21, f32[16,256,1024]{2,1,0:T(8,128)} %get-tuple-element.33, s32[]{:T(128)} %bitcast.2), kind=kOutput, calls=%fused_computation.3 | convolution fusion | flops 3221225472 | bytes 6291972 | tf_op jit(solution)/shard_map/while/body/eval_jaxpr/cond/branch_1_fun/ak,bk->ab/dot_general | solution.py:31
  247.8 1.0 constant_dynamic-update-slice_fusion.2
  249.9 8.7 %conditional.2 = (f32[1,1024,256]{2,1,0:T(8,128)S(1)}) conditional(s32[]{:T(128)} %bitcast.24, () %tuple.38, (s32[1,2]{1,0:T(1,128)S(1)}, f32[2,1024,1024]{2,1,0:T(8,128)}, f32[16,256,1024]{2,1,0:T(8,128)}) %tuple.39), branch_computations={%region_1.1_spmd, %region_2.2_spmd} | conditional | flops 3221225472 | bytes 6292042 | solution.py:44
  253.0 5.6 %fusion.3 = f32[1,1024,256]{2,1,0:T(8,128)S(1)} fusion(f32[2,1024,1024]{2,1,0:T(8,128)} %get-tuple-element.31, s32[]{:T(128)S(6)} %select_n.21, f32[16,256,1024]{2,1,0:T(8,128)} %get-tuple-element.33, s32[]{:T(128)} %bitcast.2), kind=kOutput, calls=%fused_computation.3 | convolution fusion | flops 3221225472 | bytes 6291972 | tf_op jit(solution)/shard_map/while/body/eval_jaxpr/cond/branch_1_fun/ak,bk->ab/dot_general | solution.py:31
  258.6 1.0 constant_dynamic-update-slice_fusion.2
  260.8 8.7 %conditional.2 = (f32[1,1024,256]{2,1,0:T(8,128)S(1)}) conditional(s32[]{:T(128)} %bitcast.24, () %tuple.38, (s32[1,2]{1,0:T(1,128)S(1)}, f32[2,1024,1024]{2,1,0:T(8,128)}, f32[16,256,1024]{2,1,0:T(8,128)}) %tuple.39), branch_computations={%region_1.1_spmd, %region_2.2_spmd} | conditional | flops 3221225472 | bytes 6292042 | solution.py:44
  263.9 5.6 %fusion.3 = f32[1,1024,256]{2,1,0:T(8,128)S(1)} fusion(f32[2,1024,1024]{2,1,0:T(8,128)} %get-tuple-element.31, s32[]{:T(128)S(6)} %select_n.21, f32[16,256,1024]{2,1,0:T(8,128)} %get-tuple-element.33, s32[]{:T(128)} %bitcast.2), kind=kOutput, calls=%fused_computation.3 | convolution fusion | flops 3221225472 | bytes 6291972 | tf_op jit(solution)/shard_map/while/body/eval_jaxpr/cond/branch_1_fun/ak,bk->ab/dot_general | solution.py:31
  269.5 1.0 constant_dynamic-update-slice_fusion.2
  271.6 8.7 %conditional.2 = (f32[1,1024,256]{2,1,0:T(8,128)S(1)}) conditional(s32[]{:T(128)} %bitcast.24, () %tuple.38, (s32[1,2]{1,0:T(1,128)S(1)}, f32[2,1024,1024]{2,1,0:T(8,128)}, f32[16,256,1024]{2,1,0:T(8,128)}) %tuple.39), branch_computations={%region_1.1_spmd, %region_2.2_spmd} | conditional | flops 3221225472 | bytes 6292042 | solution.py:44
  274.7 5.6 %fusion.3 = f32[1,1024,256]{2,1,0:T(8,128)S(1)} fusion(f32[2,1024,1024]{2,1,0:T(8,128)} %get-tuple-element.31, s32[]{:T(128)S(6)} %select_n.21, f32[16,256,1024]{2,1,0:T(8,128)} %get-tuple-element.33, s32[]{:T(128)} %bitcast.2), kind=kOutput, calls=%fused_computation.3 | convolution fusion | flops 3221225472 | bytes 6291972 | tf_op jit(solution)/shard_map/while/body/eval_jaxpr/cond/branch_1_fun/ak,bk->ab/dot_general | solution.py:31
  280.3 1.0 constant_dynamic-update-slice_fusion.2
  282.5 8.7 %conditional.2 = (f32[1,1024,256]{2,1,0:T(8,128)S(1)}) conditional(s32[]{:T(128)} %bitcast.24, () %tuple.38, (s32[1,2]{1,0:T(1,128)S(1)}, f32[2,1024,1024]{2,1,0:T(8,128)}, f32[16,256,1024]{2,1,0:T(8,128)}) %tuple.39), branch_computations={%region_1.1_spmd, %region_2.2_spmd} | conditional | flops 3221225472 | bytes 6292042 | solution.py:44
  285.6 5.6 %fusion.3 = f32[1,1024,256]{2,1,0:T(8,128)S(1)} fusion(f32[2,1024,1024]{2,1,0:T(8,128)} %get-tuple-element.31, s32[]{:T(128)S(6)} %select_n.21, f32[16,256,1024]{2,1,0:T(8,128)} %get-tuple-element.33, s32[]{:T(128)} %bitcast.2), kind=kOutput, calls=%fused_computation.3 | convolution fusion | flops 3221225472 | bytes 6291972 | tf_op jit(solution)/shard_map/while/body/eval_jaxpr/cond/branch_1_fun/ak,bk->ab/dot_general | solution.py:31
  291.2 1.0 constant_dynamic-update-slice_fusion.2
  293.4 8.7 %conditional.2 = (f32[1,1024,256]{2,1,0:T(8,128)S(1)}) conditional(s32[]{:T(128)} %bitcast.24, () %tuple.38, (s32[1,2]{1,0:T(1,128)S(1)}, f32[2,1024,1024]{2,1,0:T(8,128)}, f32[16,256,1024]{2,1,0:T(8,128)}) %tuple.39), branch_computations={%region_1.1_spmd, %region_2.2_spmd} | conditional | flops 3221225472 | bytes 6292042 | solution.py:44
  296.5 5.6 %fusion.3 = f32[1,1024,256]{2,1,0:T(8,128)S(1)} fusion(f32[2,1024,1024]{2,1,0:T(8,128)} %get-tuple-element.31, s32[]{:T(128)S(6)} %select_n.21, f32[16,256,1024]{2,1,0:T(8,128)} %get-tuple-element.33, s32[]{:T(128)} %bitcast.2), kind=kOutput, calls=%fused_computation.3 | convolution fusion | flops 3221225472 | bytes 6291972 | tf_op jit(solution)/shard_map/while/body/eval_jaxpr/cond/branch_1_fun/ak,bk->ab/dot_general | solution.py:31
  302.0 1.0 constant_dynamic-update-slice_fusion.2
  304.2 8.7 %conditional.2 = (f32[1,1024,256]{2,1,0:T(8,128)S(1)}) conditional(s32[]{:T(128)} %bitcast.24, () %tuple.38, (s32[1,2]{1,0:T(1,128)S(1)}, f32[2,1024,1024]{2,1,0:T(8,128)}, f32[16,256,1024]{2,1,0:T(8,128)}) %tuple.39), branch_computations={%region_1.1_spmd, %region_2.2_spmd} | conditional | flops 3221225472 | bytes 6292042 | solution.py:44
  307.3 5.6 %fusion.3 = f32[1,1024,256]{2,1,0:T(8,128)S(1)} fusion(f32[2,1024,1024]{2,1,0:T(8,128)} %get-tuple-element.31, s32[]{:T(128)S(6)} %select_n.21, f32[16,256,1024]{2,1,0:T(8,128)} %get-tuple-element.33, s32[]{:T(128)} %bitcast.2), kind=kOutput, calls=%fused_computation.3 | convolution fusion | flops 3221225472 | bytes 6291972 | tf_op jit(solution)/shard_map/while/body/eval_jaxpr/cond/branch_1_fun/ak,bk->ab/dot_general | solution.py:31
  312.9 1.0 constant_dynamic-update-slice_fusion.2
  315.1 8.7 %conditional.2 = (f32[1,1024,256]{2,1,0:T(8,128)S(1)}) conditional(s32[]{:T(128)} %bitcast.24, () %tuple.38, (s32[1,2]{1,0:T(1,128)S(1)}, f32[2,1024,1024]{2,1,0:T(8,128)}, f32[16,256,1024]{2,1,0:T(8,128)}) %tuple.39), branch_computations={%region_1.1_spmd, %region_2.2_spmd} | conditional | flops 3221225472 | bytes 6292042 | solution.py:44
  318.2 5.6 %fusion.3 = f32[1,1024,256]{2,1,0:T(8,128)S(1)} fusion(f32[2,1024,1024]{2,1,0:T(8,128)} %get-tuple-element.31, s32[]{:T(128)S(6)} %select_n.21, f32[16,256,1024]{2,1,0:T(8,128)} %get-tuple-element.33, s32[]{:T(128)} %bitcast.2), kind=kOutput, calls=%fused_computation.3 | convolution fusion | flops 3221225472 | bytes 6291972 | tf_op jit(solution)/shard_map/while/body/eval_jaxpr/cond/branch_1_fun/ak,bk->ab/dot_general | solution.py:31
  326.0 8.7 %conditional.2 = (f32[1,1024,256]{2,1,0:T(8,128)S(1)}) conditional(s32[]{:T(128)} %bitcast.24, () %tuple.38, (s32[1,2]{1,0:T(1,128)S(1)}, f32[2,1024,1024]{2,1,0:T(8,128)}, f32[16,256,1024]{2,1,0:T(8,128)}) %tuple.39), branch_computations={%region_1.1_spmd, %region_2.2_spmd} | conditional | flops 3221225472 | bytes 6292042 | solution.py:44
  329.0 5.6 %fusion.3 = f32[1,1024,256]{2,1,0:T(8,128)S(1)} fusion(f32[2,1024,1024]{2,1,0:T(8,128)} %get-tuple-element.31, s32[]{:T(128)S(6)} %select_n.21, f32[16,256,1024]{2,1,0:T(8,128)} %get-tuple-element.33, s32[]{:T(128)} %bitcast.2), kind=kOutput, calls=%fused_computation.3 | convolution fusion | flops 3221225472 | bytes 6291972 | tf_op jit(solution)/shard_map/while/body/eval_jaxpr/cond/branch_1_fun/ak,bk->ab/dot_general | solution.py:31
  336.8 8.7 %conditional.2 = (f32[1,1024,256]{2,1,0:T(8,128)S(1)}) conditional(s32[]{:T(128)} %bitcast.24, () %tuple.38, (s32[1,2]{1,0:T(1,128)S(1)}, f32[2,1024,1024]{2,1,0:T(8,128)}, f32[16,256,1024]{2,1,0:T(8,128)}) %tuple.39), branch_computations={%region_1.1_spmd, %region_2.2_spmd} | conditional | flops 3221225472 | bytes 6292042 | solution.py:44
  339.9 5.6 %fusion.3 = f32[1,1024,256]{2,1,0:T(8,128)S(1)} fusion(f32[2,1024,1024]{2,1,0:T(8,128)} %get-tuple-element.31, s32[]{:T(128)S(6)} %select_n.21, f32[16,256,1024]{2,1,0:T(8,128)} %get-tuple-element.33, s32[]{:T(128)} %bitcast.2), kind=kOutput, calls=%fused_computation.3 | convolution fusion | flops 3221225472 | bytes 6291972 | tf_op jit(solution)/shard_map/while/body/eval_jaxpr/cond/branch_1_fun/ak,bk->ab/dot_general | solution.py:31
  345.5 1.0 constant_dynamic-update-slice_fusion.2
  347.7 8.7 %conditional.2 = (f32[1,1024,256]{2,1,0:T(8,128)S(1)}) conditional(s32[]{:T(128)} %bitcast.24, () %tuple.38, (s32[1,2]{1,0:T(1,128)S(1)}, f32[2,1024,1024]{2,1,0:T(8,128)}, f32[16,256,1024]{2,1,0:T(8,128)}) %tuple.39), branch_computations={%region_1.1_spmd, %region_2.2_spmd} | conditional | flops 3221225472 | bytes 6292042 | solution.py:44
  350.8 5.6 %fusion.3 = f32[1,1024,256]{2,1,0:T(8,128)S(1)} fusion(f32[2,1024,1024]{2,1,0:T(8,128)} %get-tuple-element.31, s32[]{:T(128)S(6)} %select_n.21, f32[16,256,1024]{2,1,0:T(8,128)} %get-tuple-element.33, s32[]{:T(128)} %bitcast.2), kind=kOutput, calls=%fused_computation.3 | convolution fusion | flops 3221225472 | bytes 6291972 | tf_op jit(solution)/shard_map/while/body/eval_jaxpr/cond/branch_1_fun/ak,bk->ab/dot_general | solution.py:31
  358.5 8.7 %conditional.2 = (f32[1,1024,256]{2,1,0:T(8,128)S(1)}) conditional(s32[]{:T(128)} %bitcast.24, () %tuple.38, (s32[1,2]{1,0:T(1,128)S(1)}, f32[2,1024,1024]{2,1,0:T(8,128)}, f32[16,256,1024]{2,1,0:T(8,128)}) %tuple.39), branch_computations={%region_1.1_spmd, %region_2.2_spmd} | conditional | flops 3221225472 | bytes 6292042 | solution.py:44
  361.6 5.6 %fusion.3 = f32[1,1024,256]{2,1,0:T(8,128)S(1)} fusion(f32[2,1024,1024]{2,1,0:T(8,128)} %get-tuple-element.31, s32[]{:T(128)S(6)} %select_n.21, f32[16,256,1024]{2,1,0:T(8,128)} %get-tuple-element.33, s32[]{:T(128)} %bitcast.2), kind=kOutput, calls=%fused_computation.3 | convolution fusion | flops 3221225472 | bytes 6291972 | tf_op jit(solution)/shard_map/while/body/eval_jaxpr/cond/branch_1_fun/ak,bk->ab/dot_general | solution.py:31
  369.4 8.7 %conditional.2 = (f32[1,1024,256]{2,1,0:T(8,128)S(1)}) conditional(s32[]{:T(128)} %bitcast.24, () %tuple.38, (s32[1,2]{1,0:T(1,128)S(1)}, f32[2,1024,1024]{2,1,0:T(8,128)}, f32[16,256,1024]{2,1,0:T(8,128)}) %tuple.39), branch_computations={%region_1.1_spmd, %region_2.2_spmd} | conditional | flops 3221225472 | bytes 6292042 | solution.py:44
  372.5 5.6 %fusion.3 = f32[1,1024,256]{2,1,0:T(8,128)S(1)} fusion(f32[2,1024,1024]{2,1,0:T(8,128)} %get-tuple-element.31, s32[]{:T(128)S(6)} %select_n.21, f32[16,256,1024]{2,1,0:T(8,128)} %get-tuple-element.33, s32[]{:T(128)} %bitcast.2), kind=kOutput, calls=%fused_computation.3 | convolution fusion | flops 3221225472 | bytes 6291972 | tf_op jit(solution)/shard_map/while/body/eval_jaxpr/cond/branch_1_fun/ak,bk->ab/dot_general | solution.py:31
  380.3 8.7 %conditional.2 = (f32[1,1024,256]{2,1,0:T(8,128)S(1)}) conditional(s32[]{:T(128)} %bitcast.24, () %tuple.38, (s32[1,2]{1,0:T(1,128)S(1)}, f32[2,1024,1024]{2,1,0:T(8,128)}, f32[16,256,1024]{2,1,0:T(8,128)}) %tuple.39), branch_computations={%region_1.1_spmd, %region_2.2_spmd} | conditional | flops 3221225472 | bytes 6292042 | solution.py:44
  383.4 5.6 %fusion.3 = f32[1,1024,256]{2,1,0:T(8,128)S(1)} fusion(f32[2,1024,1024]{2,1,0:T(8,128)} %get-tuple-element.31, s32[]{:T(128)S(6)} %select_n.21, f32[16,256,1024]{2,1,0:T(8,128)} %get-tuple-element.33, s32[]{:T(128)} %bitcast.2), kind=kOutput, calls=%fused_computation.3 | convolution fusion | flops 3221225472 | bytes 6291972 | tf_op jit(solution)/shard_map/while/body/eval_jaxpr/cond/branch_1_fun/ak,bk->ab/dot_general | solution.py:31
  388.9 1.0 constant_dynamic-update-slice_fusion.2
  391.1 8.7 %conditional.2 = (f32[1,1024,256]{2,1,0:T(8,128)S(1)}) conditional(s32[]{:T(128)} %bitcast.24, () %tuple.38, (s32[1,2]{1,0:T(1,128)S(1)}, f32[2,1024,1024]{2,1,0:T(8,128)}, f32[16,256,1024]{2,1,0:T(8,128)}) %tuple.39), branch_computations={%region_1.1_spmd, %region_2.2_spmd} | conditional | flops 3221225472 | bytes 6292042 | solution.py:44
  394.2 5.6 %fusion.3 = f32[1,1024,256]{2,1,0:T(8,128)S(1)} fusion(f32[2,1024,1024]{2,1,0:T(8,128)} %get-tuple-element.31, s32[]{:T(128)S(6)} %select_n.21, f32[16,256,1024]{2,1,0:T(8,128)} %get-tuple-element.33, s32[]{:T(128)} %bitcast.2), kind=kOutput, calls=%fused_computation.3 | convolution fusion | flops 3221225472 | bytes 6291972 | tf_op jit(solution)/shard_map/while/body/eval_jaxpr/cond/branch_1_fun/ak,bk->ab/dot_general | solution.py:31
  399.8 1.0 constant_dynamic-update-slice_fusion.2
  402.0 8.7 %conditional.2 = (f32[1,1024,256]{2,1,0:T(8,128)S(1)}) conditional(s32[]{:T(128)} %bitcast.24, () %tuple.38, (s32[1,2]{1,0:T(1,128)S(1)}, f32[2,1024,1024]{2,1,0:T(8,128)}, f32[16,256,1024]{2,1,0:T(8,128)}) %tuple.39), branch_computations={%region_1.1_spmd, %region_2.2_spmd} | conditional | flops 3221225472 | bytes 6292042 | solution.py:44
  405.1 5.6 %fusion.3 = f32[1,1024,256]{2,1,0:T(8,128)S(1)} fusion(f32[2,1024,1024]{2,1,0:T(8,128)} %get-tuple-element.31, s32[]{:T(128)S(6)} %select_n.21, f32[16,256,1024]{2,1,0:T(8,128)} %get-tuple-element.33, s32[]{:T(128)} %bitcast.2), kind=kOutput, calls=%fused_computation.3 | convolution fusion | flops 3221225472 | bytes 6291972 | tf_op jit(solution)/shard_map/while/body/eval_jaxpr/cond/branch_1_fun/ak,bk->ab/dot_general | solution.py:31
  412.8 8.7 %conditional.2 = (f32[1,1024,256]{2,1,0:T(8,128)S(1)}) conditional(s32[]{:T(128)} %bitcast.24, () %tuple.38, (s32[1,2]{1,0:T(1,128)S(1)}, f32[2,1024,1024]{2,1,0:T(8,128)}, f32[16,256,1024]{2,1,0:T(8,128)}) %tuple.39), branch_computations={%region_1.1_spmd, %region_2.2_spmd} | conditional | flops 3221225472 | bytes 6292042 | solution.py:44
  415.9 5.6 %fusion.3 = f32[1,1024,256]{2,1,0:T(8,128)S(1)} fusion(f32[2,1024,1024]{2,1,0:T(8,128)} %get-tuple-element.31, s32[]{:T(128)S(6)} %select_n.21, f32[16,256,1024]{2,1,0:T(8,128)} %get-tuple-element.33, s32[]{:T(128)} %bitcast.2), kind=kOutput, calls=%fused_computation.3 | convolution fusion | flops 3221225472 | bytes 6291972 | tf_op jit(solution)/shard_map/while/body/eval_jaxpr/cond/branch_1_fun/ak,bk->ab/dot_general | solution.py:31
  423.7 8.7 %conditional.2 = (f32[1,1024,256]{2,1,0:T(8,128)S(1)}) conditional(s32[]{:T(128)} %bitcast.24, () %tuple.38, (s32[1,2]{1,0:T(1,128)S(1)}, f32[2,1024,1024]{2,1,0:T(8,128)}, f32[16,256,1024]{2,1,0:T(8,128)}) %tuple.39), branch_computations={%region_1.1_spmd, %region_2.2_spmd} | conditional | flops 3221225472 | bytes 6292042 | solution.py:44
  426.8 5.6 %fusion.3 = f32[1,1024,256]{2,1,0:T(8,128)S(1)} fusion(f32[2,1024,1024]{2,1,0:T(8,128)} %get-tuple-element.31, s32[]{:T(128)S(6)} %select_n.21, f32[16,256,1024]{2,1,0:T(8,128)} %get-tuple-element.33, s32[]{:T(128)} %bitcast.2), kind=kOutput, calls=%fused_computation.3 | convolution fusion | flops 3221225472 | bytes 6291972 | tf_op jit(solution)/shard_map/while/body/eval_jaxpr/cond/branch_1_fun/ak,bk->ab/dot_general | solution.py:31
  434.6 8.7 %conditional.2 = (f32[1,1024,256]{2,1,0:T(8,128)S(1)}) conditional(s32[]{:T(128)} %bitcast.24, () %tuple.38, (s32[1,2]{1,0:T(1,128)S(1)}, f32[2,1024,1024]{2,1,0:T(8,128)}, f32[16,256,1024]{2,1,0:T(8,128)}) %tuple.39), branch_computations={%region_1.1_spmd, %region_2.2_spmd} | conditional | flops 3221225472 | bytes 6292042 | solution.py:44
  437.6 5.6 %fusion.3 = f32[1,1024,256]{2,1,0:T(8,128)S(1)} fusion(f32[2,1024,1024]{2,1,0:T(8,128)} %get-tuple-element.31, s32[]{:T(128)S(6)} %select_n.21, f32[16,256,1024]{2,1,0:T(8,128)} %get-tuple-element.33, s32[]{:T(128)} %bitcast.2), kind=kOutput, calls=%fused_computation.3 | convolution fusion | flops 3221225472 | bytes 6291972 | tf_op jit(solution)/shard_map/while/body/eval_jaxpr/cond/branch_1_fun/ak,bk->ab/dot_general | solution.py:31
  444.3 21.9 %sub.3 = f32[20,1024,256]{2,1,0:T(8,128)} subtract(f32[20,1024,256]{2,1,0:T(8,128)} %param.10, f32[20,1024,256]{2,1,0:T(8,128)} %get-tuple-element.43) | non-fusion elementwise | flops 5242880 | bytes 62914560 | tf_op jit(solution)/shard_map/sub | solution.py:51
  (84 shorter events, 33.4 us)
Async XLA Ops:
  7.2 49.6 %copy-start = (f32[2,256,1024]{2,1,0:T(8,128)S(1)}, f32[2,256,1024]{2,1,0:T(8,128)}, u32[]{:S(2)}) copy-start(f32[2,256,1024]{2,1,0:T(8,128)} %param.9) | copy-start | bytes 6291460
  7.2 49.6 %all-gather.3.cloned.1.call-start = ((), (), s32[]{:S(2)}) async-start(), calls=%async_computation | async-start | bytes 4718592 | tf_op jit(solution)/shard_map/all_gather | solution.py:35
  7.9 219.2 %all-gather.5.cloned.1.call-start = ((), (), s32[]{:S(2)}) async-start(), calls=%async_computation.1 | async-start | bytes 18874368 | tf_op jit(solution)/shard_map/all_gather | solution.py:40
  66.4 47.3 %collective-permute-start = (f32[1,2,256,1024]{3,2,1,0:T(8,128)}, f32[1,2,256,1024]{3,2,1,0:T(8,128)}, u32[]{:S(2)}, u32[]{:S(2)}) collective-permute-start(f32[1,2,256,1024]{3,2,1,0:T(8,128)} %bitcast.26), channel_id=1, source_target_pairs={{0,1},{1,0},{2,3},{3,2},{4,5},{5,4},{6,7},{7,6},{8,9},{9,8},{10,11... | collective-permute-start | bytes 6291464 | tf_op jit(solution)/shard_map/ppermute | solution.py:19
  116.6 2.7 copy-start.2
  116.6 3.9 copy-start.3
  119.3 91.3 %collective-permute-start.1 = (f32[2,2,256,1024]{3,2,1,0:T(8,128)}, f32[2,2,256,1024]{3,2,1,0:T(8,128)}, u32[]{:S(2)}, u32[]{:S(2)}) collective-permute-start(f32[2,2,256,1024]{3,2,1,0:T(8,128)} %pad_maximum_fusion), channel_id=1, source_target_pairs={{0,2},{1,3},{2,0},{3,1},{4,6},{5,7},{6,4},{7,5},{8,10},{9,11},{10,... | collective-permute-start | bytes 12582920 | tf_op jit(solution)/shard_map/ppermute | solution.py:19
  444.3 21.9 %copy-start.1 = (f32[2,256,1024]{2,1,0:T(8,128)S(1)}, f32[2,256,1024]{2,1,0:T(8,128)}, u32[]{:S(2)}) copy-start(f32[2,256,1024]{2,1,0:T(8,128)} %param.9) | copy-start | bytes 6291460
Sparse Core Ops, SparseCore 0:
  9.6 47.1 all-gather.2
  66.6 149.2 all-gather.4
